TPU v7x, 32 devices: a whole 2x2x4 slice. The times are simulated.
32 devices in a mesh: replica: 8 (over y, x, core), group: 4 (over z).
Axes of the slice: x: 2, y: 2, z: 4, core: 2. Of those that a mesh axis runs over, the one named last changes fastest.
Arguments:
- inputs: bfloat16 [8, 512, 2048], P('replica', 'group'), may hold values from -6 to 6
- seq_lengths: int32 [8], P('replica'), may hold values from 128 to 512, as said below
- bucket_ids: int32 [1023], replicated, may hold values from 0 to 31, as said below
- norm1_gain: bfloat16 [2048], P('group'), may hold values from 0.25 to 1.75
- w_query: bfloat16 [2048, 2048], P(None, 'group'), may hold values from -0.0625 to 0.0625
- w_key: bfloat16 [2048, 2048], P(None, 'group'), may hold values from -0.0625 to 0.0625
- w_value: bfloat16 [2048, 2048], P(None, 'group'), may hold values from -0.125 to 0.125
- w_attn_out: bfloat16 [2048, 2048], P('group'), may hold values from -0.5 to 0.5
- bias_table: bfloat16 [32, 32], P(None, 'group'), may hold values from -4 to 4
- norm2_gain: bfloat16 [2048], P('group'), may hold values from 0.25 to 1.75
- w_gate: bfloat16 [2048, 5120], P(None, 'group'), may hold values from -0.125 to 0.125
- w_up: bfloat16 [2048, 5120], P(None, 'group'), may hold values from -0.125 to 0.125
- w_ffn_out: bfloat16 [5120, 2048], P('group'), may hold values from -0.078125 to 0.078125
- cotangent: bfloat16 [8, 512, 2048], P('replica', 'group'), may hold values from -6 to 6
Outputs:
- result: bfloat16 [8, 512, 2048], P('replica', 'group')
- input_grad: bfloat16 [8, 512, 2048], P('replica', 'group')
- norm1_gain_grad: float32 [2048], P('group')
- query_grad: float32 [2048, 2048], P(None, 'group')
- key_grad: float32 [2048, 2048], P(None, 'group')
- value_grad: float32 [2048, 2048], P(None, 'group')
- attn_out_grad: float32 [2048, 2048], P('group')
- bias_table_grad: float32 [32, 32], P(None, 'group')
- norm2_gain_grad: float32 [2048], P('group')
- gate_grad: float32 [2048, 5120], P(None, 'group')
- up_grad: float32 [2048, 5120], P(None, 'group')
- ffn_out_grad: float32 [5120, 2048], P('group')
Inputs may be any that keep to these rules, and one draw needn't show every extreme that they name: `seq_lengths`: one sequence has exactly 512 valid positions and another exactly 128. `bucket_ids`: entry 511 + o is the bucket of the offset o = key position - query position; every bucket occurs.
All inputs are finite; a program needn't handle non-finite values.
Results may differ from a plain program's by a relative error of at most 0.02.
Values may be sent and summed in bfloat16 or wider, within the bound.
A program may use at most 448 MiB of HBM per device.

v0:
```python
import jax
import jax.numpy as jnp
from jax import lax
from jax.sharding import PartitionSpec as P

epsilon = 1e-06
negative = -1000000000.0
highest = lax.Precision.HIGHEST
head_dim = 64


def rms_scale(values, gain):
    return values * lax.rsqrt(jnp.mean(values * values, axis=-1, keepdims=True) + epsilon) * gain


def gated_gelu(gate_pre, up_pre):
    return jax.nn.gelu(gate_pre, approximate=True) * up_pre


def rows_dot(left, right):
    return lax.dot_general(
        left, right, (((0,), (0,)), ((), ())), preferred_element_type=jnp.float32
    )


def cols_dot(left, right):
    return lax.dot_general(
        left, right, (((1,), (1,)), ((), ())), preferred_element_type=jnp.float32
    )


def plain_dot(left, right):
    return jnp.dot(left, right, preferred_element_type=jnp.float32)


def spread_offsets(vector, row_count, col_count):
    span_width = row_count + col_count + 1
    block_heads = vector.shape[0]
    tiled_rows = jnp.broadcast_to(vector[:, None, :], (block_heads, row_count, span_width))
    flattened = tiled_rows.reshape(block_heads, row_count * span_width)[
        :, : row_count * (span_width - 1)
    ]
    return flattened.reshape(block_heads, row_count, span_width - 1)[:, :, row_count:]


def fold_offsets(matrix):
    block_heads, row_count, col_count = matrix.shape
    padded = jnp.pad(matrix, ((0, 0), (0, 0), (row_count, 0)))
    flattened = jnp.pad(
        padded.reshape(block_heads, row_count * (row_count + col_count)), ((0, 0), (0, row_count))
    )
    sums_all = flattened.reshape(block_heads, row_count, row_count + col_count + 1).sum(axis=1)
    return sums_all[:, 1 : row_count + col_count]


def heads(matrix):
    return matrix.reshape(matrix.shape[0], -1, head_dim)


def local(
    inputs,
    seq_lengths,
    bucket_ids,
    norm1_gain,
    w_query,
    w_key,
    w_value,
    w_attn_out,
    bias_table,
    norm2_gain,
    w_gate,
    w_up,
    w_ffn_out,
    cotangent,
):
    group = lax.axis_index("group")
    rows = inputs.shape[1]
    length = seq_lengths[0]
    total = rows * lax.axis_size("group")
    start = group * rows
    valid = jnp.arange(total) < length

    def gather(values):
        return lax.all_gather(values, "group", axis=0, tiled=True)

    def scatter(values):
        return lax.psum_scatter(
            values.astype(jnp.bfloat16), "group", scatter_dimension=0, tiled=True
        ).astype(jnp.float32)

    x_all_low = gather(inputs[0])
    g_all = jnp.where(valid[:, None], gather(cotangent[0]), jnp.bfloat16(0))
    gains = lax.all_gather(jnp.stack([norm1_gain, norm2_gain]), "group", axis=1, tiled=True)
    gains = gains.astype(jnp.float32)
    gain_first, gain_second = (gains[0], gains[1])
    x_local = inputs[0].astype(jnp.float32)
    normed_one = rms_scale(x_all_low.astype(jnp.float32), gain_first).astype(jnp.bfloat16)
    query = plain_dot(normed_one, w_query).astype(jnp.bfloat16)
    key = plain_dot(normed_one, w_key).astype(jnp.bfloat16)
    value = plain_dot(normed_one, w_value).astype(jnp.bfloat16)
    buckets = bias_table.shape[0]
    one_hot = (bucket_ids[:, None] == jnp.arange(buckets)[None, :]).astype(jnp.float32)
    per_offset = jnp.dot(one_hot, bias_table.astype(jnp.float32), precision=highest)
    bias = spread_offsets(jnp.pad(per_offset.T, ((0, 0), (1, 1))), total, total)
    scores = jnp.einsum(
        "qhd,khd->hqk", heads(query), heads(key), preferred_element_type=jnp.float32
    )
    scores = jnp.where(valid[None, None, :], scores + bias, negative)
    probs = jax.nn.softmax(scores, axis=-1)
    probs_low = probs.astype(jnp.bfloat16)
    attended = jnp.einsum(
        "hqk,khd->qhd", probs_low, heads(value), preferred_element_type=jnp.float32
    )
    attended = attended.reshape(total, -1).astype(jnp.bfloat16)
    middle = x_local + scatter(plain_dot(attended, w_attn_out))
    normed_two = gather(rms_scale(middle, gain_second).astype(jnp.bfloat16))
    gate_pre = plain_dot(normed_two, w_gate)
    up_pre = plain_dot(normed_two, w_up)
    hidden_low = gated_gelu(gate_pre, up_pre).astype(jnp.bfloat16)
    grad_hidden = cols_dot(g_all, w_ffn_out)
    _, pull_gelu = jax.vjp(gated_gelu, gate_pre, up_pre)
    grad_gate, grad_up = pull_gelu(grad_hidden)
    grad_gate = grad_gate.astype(jnp.bfloat16)
    grad_up = grad_up.astype(jnp.bfloat16)
    grad_normed_two = scatter(cols_dot(grad_gate, w_gate) + cols_dot(grad_up, w_up))
    ffn_out_grad = rows_dot(hidden_low, g_all)
    gate_grad = rows_dot(normed_two, grad_gate)
    up_grad = rows_dot(normed_two, grad_up)

    def total_sum(values):
        return lax.psum(values.astype(jnp.bfloat16), "replica").astype(jnp.float32)

    ffn_out_grad, gate_grad, up_grad = (
        total_sum(ffn_out_grad),
        total_sum(gate_grad),
        total_sum(up_grad),
    )
    result = (middle + scatter(plain_dot(hidden_low, w_ffn_out))).astype(jnp.bfloat16)
    row_valid = start + jnp.arange(rows) < length
    g_local = jnp.where(row_valid[:, None], cotangent[0], jnp.bfloat16(0)).astype(jnp.float32)
    _, pull_two = jax.vjp(rms_scale, middle, gain_second)
    grad_mid_norm, gain_two_grad = pull_two(grad_normed_two)
    grad_middle = g_local + grad_mid_norm
    grad_branch = gather(grad_middle.astype(jnp.bfloat16))
    attn_out_grad = rows_dot(attended, grad_branch)
    grad_attended = cols_dot(grad_branch, w_attn_out).astype(jnp.bfloat16)
    grad_probs = jnp.einsum(
        "qhd,khd->hqk", heads(grad_attended), heads(value), preferred_element_type=jnp.float32
    )
    inner_sum = jnp.sum(probs * grad_probs, axis=-1, keepdims=True)
    grad_scores = (probs * (grad_probs - inner_sum)).astype(jnp.bfloat16)

    def merge(values):
        return values.reshape(total, -1).astype(jnp.bfloat16)

    grad_query = merge(
        jnp.einsum("hqk,khd->qhd", grad_scores, heads(key), preferred_element_type=jnp.float32)
    )
    grad_key = merge(
        jnp.einsum("hqk,qhd->khd", grad_scores, heads(query), preferred_element_type=jnp.float32)
    )
    grad_value = merge(
        jnp.einsum(
            "hqk,qhd->khd", probs_low, heads(grad_attended), preferred_element_type=jnp.float32
        )
    )
    offset_sums = fold_offsets(grad_scores.astype(jnp.float32))
    table_grad = jnp.dot(offset_sums, one_hot, precision=highest).T
    query_grad = rows_dot(normed_one, grad_query)
    key_grad = rows_dot(normed_one, grad_key)
    value_grad = rows_dot(normed_one, grad_value)
    grad_normed_one = scatter(
        cols_dot(grad_query, w_query) + cols_dot(grad_key, w_key) + cols_dot(grad_value, w_value)
    )
    query_grad, key_grad, value_grad, attn_out_grad = (
        total_sum(query_grad),
        total_sum(key_grad),
        total_sum(value_grad),
        total_sum(attn_out_grad),
    )
    table_grad = lax.psum(table_grad, "replica")
    _, pull_one = jax.vjp(rms_scale, x_local, gain_first)
    grad_in_norm, gain_one_grad = pull_one(grad_normed_one)
    input_grad = (grad_middle + grad_in_norm).astype(jnp.bfloat16)
    gain_sums = lax.psum(jnp.stack([gain_one_grad, gain_two_grad]), ("replica", "group"))
    width = norm1_gain.shape[0]
    gain_sums = lax.dynamic_slice_in_dim(gain_sums, group * width, width, axis=1)
    return (
        result[None],
        input_grad[None],
        gain_sums[0],
        query_grad,
        key_grad,
        value_grad,
        attn_out_grad,
        table_grad,
        gain_sums[1],
        gate_grad,
        up_grad,
        ffn_out_grad,
    )


def solution(mesh):
    placed = (
        P("replica", "group", None),
        P("replica"),
        P(),
        P("group"),
        P(None, "group"),
        P(None, "group"),
        P(None, "group"),
        P("group", None),
        P(None, "group"),
        P("group"),
        P(None, "group"),
        P(None, "group"),
        P("group", None),
        P("replica", "group", None),
    )
    return jax.shard_map(
        local,
        mesh=mesh,
        in_specs=placed,
        out_specs=(
            P("replica", "group", None),
            P("replica", "group", None),
            P("group"),
            P(None, "group"),
            P(None, "group"),
            P(None, "group"),
            P("group", None),
            P(None, "group"),
            P("group"),
            P(None, "group"),
            P(None, "group"),
            P("group", None),
        ),
        check_vma=False,
    )
```

profile of v0, /device:TPU:0, one launch (start us, length us, event | category | flops | bytes accessed | tf_op | source)
XLA Modules:
  0.0 854.6 jit_solution(4421860915725678596)
XLA Ops:
  11.1 7.7 broadcast_in_dim.67
  18.7 25.5 %reshape.150 = f32[4198400]{0:T(1024)} reshape(f32[8,512,1025]{2,1,0:T(8,128)} %broadcast_in_dim.67) | data formatting | bytes 33587200
  44.2 16.5 %reshape.135 = f32[8,524800]{1,0:T(8,128)} reshape(f32[4198400]{0:T(1024)} %reshape.150) | data formatting | bytes 33587200 | tf_op jit(solution)/shard_map/reshape | solution.py:40
  60.7 5.8 slice-done
  66.5 16.0 %copy.45 = f32[1,8,512,1024]{3,2,1,0:T(8,128)S(1)} copy(f32[1,8,512,1024]{3,1,2,0:T(8,128)S(1)} %bitcast.126) | data formatting | bytes 33554432
  82.5 4.4 slice.30
  86.9 9.1 %copy.40 = f32[8,512,512]{1,2,0:T(8,128)} copy(f32[8,512,512]{2,1,0:T(8,128)} %slice.30) | data formatting | bytes 16777216
  96.0 14.0 %all_gather.16 = bf16[2,2048]{1,0:T(2,128)(2,1)S(1)} all-gather(bf16[2,512]{1,0:T(2,128)(2,1)S(1)} %pad_maximum_fusion.1), channel_id=1, replica_groups=mesh['replica'=8,'group'=4] {'group'}, dimensions={1}, use_global_device_ids=true | all-gather | bytes 10240 | tf_op jit(solution)/shard_map/all_gather | solution.py:93
  110.1 2.2 fusion.1
  112.4 3.8 convolution_convert_fusion.13
  116.2 1.4 convolution_convert_fusion.12
  118.6 1.9 add_select_fusion
  120.6 5.0 fusion.52
  126.7 1.4 convolution_convert_fusion.14
  128.1 8.1 fusion.15
  136.3 2.6 convolution_convert_fusion.8
  138.9 43.8 %reduce-scatter.5.cloned.1.call-done = bf16[128,2048]{1,0:T(8,128)(2,1)} async-done(((bf16[512,2048]{1,0:T(8,128)(2,1)}), bf16[128,2048]{1,0:T(8,128)(2,1)}) %reduce-scatter.5.cloned.1.call-update) | async-done | bytes 524304 | tf_op jit(solution)/shard_map/reduce_scatter | solution.py:87
  184.0 2.0 multiply_convert_fusion.3
  186.9 44.6 %all-gather.7.cloned.1.call-done = bf16[512,2048]{1,0:T(8,128)(2,1)} async-done(((bf16[128,2048]{1,0:T(8,128)(2,1)}), bf16[512,2048]{1,0:T(8,128)(2,1)}) %all-gather.7.cloned.1.call-update) | async-done | bytes 2097168 | tf_op jit(solution)/shard_map/all_gather | solution.py:84
  231.5 7.6 fusion.53
  239.1 7.1 fusion.54
  246.2 31.5 %all-gather.13.cloned.1.call-done = bf16[1,512,2048]{2,1,0:T(8,128)(2,1)} async-done(((bf16[1,128,2048]{2,1,0:T(8,128)(2,1)}), bf16[1,512,2048]{2,1,0:T(8,128)(2,1)}) %all-gather.13.cloned.1.call-update) | async-done | bytes 2097168 | tf_op jit(solution)/shard_map/all_gather | solution.py:84
  277.7 10.4 %multiply_convert_fusion.1 = (bf16[512,1280]{1,0:T(8,128)(2,1)S(1)}, bf16[512,1280]{1,0:T(8,128)(2,1)S(1)}, bf16[512,1280]{1,0:T(8,128)(2,1)}) fusion(f32[512,1280]{1,0:T(8,128)} %fusion.53, f32[512,1280]{1,0:T(8,128)} %fusion.54, bf16[1280,2048]{1,0:T(8,128)(2,1)} %param.26, bf16[1,512,2048]{2,1,0:T(8,128)(2,1)} %all-gather.13.cloned.1.call-done, ...), kind=kOutput, calls=%fused_computation.34 | convolution fusion | flops 2702442496 | bytes 16515584 | tf_op jit(solution)/shard_map/dot_general | solution.py:27
  288.1 5.8 fusion.55
  293.9 6.7 add_convert_fusion.1
  300.7 42.6 %reduce-scatter.9.cloned.1.call-done = bf16[128,2048]{1,0:T(8,128)(2,1)} async-done(((bf16[512,2048]{1,0:T(8,128)(2,1)}), bf16[128,2048]{1,0:T(8,128)(2,1)}) %reduce-scatter.9.cloned.1.call-update) | async-done | bytes 524304 | tf_op jit(solution)/shard_map/reduce_scatter | solution.py:87
  343.3 1.7 fusion.25
  345.0 2.4 fusion.43
  347.7 45.2 %all-gather.9.cloned.1.call-done = bf16[512,2048]{1,0:T(8,128)(2,1)} async-done(((bf16[128,2048]{1,0:T(8,128)(2,1)}), bf16[512,2048]{1,0:T(8,128)(2,1)}) %all-gather.9.cloned.1.call-update) | async-done | bytes 2097168 | tf_op jit(solution)/shard_map/all_gather | solution.py:84
  392.9 3.7 convolution_convert_fusion.11
  396.5 8.2 fusion.18
  404.8 4.8 multiply_reduce_fusion
  410.6 2.5 multiply_convert_fusion
  413.2 1.4 convolution_convert_fusion.9
  416.8 1.3 fusion.57
  418.4 1.3 fusion.56
  419.9 2.7 add_convert_fusion
  423.1 7.1 convolution_convert_fusion.7
  430.3 7.3 convolution_convert_fusion.1
  437.7 4.7 convolution_convert_fusion.2
  442.4 4.8 convolution_convert_fusion
  447.1 6.6 copy.41
  453.7 6.7 pad_bitcast_fusion
  460.5 11.7 %copy.43 = bf16[1,8,512,1024]{3,1,2,0:T(8,128)(2,1)} copy(bf16[1,8,512,1024]{3,2,1,0:T(8,128)(2,1)} %pad_bitcast_fusion) | data formatting | bytes 16777216
  472.1 2.6 convolution_convert_fusion.3
  474.8 2.9 convolution_convert_fusion.4
  477.7 2.9 convolution_convert_fusion.5
  480.5 2.9 convolution_convert_fusion.6
  483.4 10.1 %pad_convert_fusion = f32[8,524800]{1,0:T(8,128)} fusion(bf16[8,524288]{1,0:T(8,128)(2,1)} %bitcast.132), kind=kLoop, calls=%fused_computation.2 | loop fusion | flops 4198400 | bytes 25182208 | tf_op jit(solution)/shard_map/reshape | solution.py:52
  493.5 12.7 %reshape.152 = f32[4198400]{0:T(1024)} reshape(f32[8,524800]{1,0:T(8,128)} %pad_convert_fusion) | data formatting | bytes 33587200
  506.2 31.4 %reshape.144 = f32[8,512,1025]{2,1,0:T(8,128)} reshape(f32[4198400]{0:T(1024)} %reshape.152) | data formatting | bytes 33587200 | tf_op jit(solution)/shard_map/reshape | solution.py:52
  537.6 7.7 reduce_sum.104
  545.7 13.8 %psum.68 = f32[32,8]{0,1:T(8,128)} all-reduce(f32[32,8]{0,1:T(8,128)S(1)} %fusion.35), channel_id=1, replica_groups=mesh['replica'=8,'group'=4] {'replica'}, use_global_device_ids=true, to_apply=%region_20.21 | all-reduce | flops 256 | bytes 2048 | tf_op jit(solution)/shard_map/psum | solution.py:181
  559.5 1.6 fusion.26
  561.2 39.4 %psum.63 = f32[2,2048]{1,0:T(2,128)S(1)} all-reduce(f32[2,2048]{1,0:T(2,128)S(1)} %pad_maximum_fusion), channel_id=1, replica_groups=mesh['replica'=8,'group'=4] {'replica','group'}, use_global_device_ids=true, to_apply=%region_14.15 | all-reduce | flops 4096 | bytes 32768 | tf_op jit(solution)/shard_map/psum | solution.py:185
  601.3 3.3 fusion.34
  604.5 214.6 %all-reduce.6.cloned.1.call-done = (bf16[2048,512]{1,0:T(8,128)(2,1)}, bf16[2048,512]{1,0:T(8,128)(2,1)}, bf16[2048,512]{1,0:T(8,128)(2,1)}, bf16[512,2048]{1,0:...) async-done(((bf16[2048,512]{1,0:T(8,128)(2,1)}, bf16[2048,512]{1,0:T(8,128)(2,1)}, bf16[2048,512]{1,0:T(8,128)(2,1)}, ...) | async-done | bytes 24117264 | tf_op jit(solution)/shard_map/psum | solution.py:131
  819.1 7.9 convert_element_type.212
  827.0 4.9 convert_element_type.214
  831.9 5.5 convert_element_type.216
  837.4 2.6 convert_element_type.204
  840.1 2.6 convert_element_type.206
  842.7 2.6 convert_element_type.208
  845.3 2.5 convert_element_type.210
  (131 shorter events, 13.3 us)
Async XLA Ops:
  7.2 129.1 %copy-start = (bf16[512,2048]{1,0:T(8,128)(2,1)S(1)}, bf16[512,2048]{1,0:T(8,128)(2,1)}, u32[]{:S(2)}) copy-start(bf16[512,2048]{1,0:T(8,128)(2,1)} %param.21) | copy-start | bytes 6291460
  7.2 102.9 %all-gather.11.cloned.1.call-start = ((), (), s32[]{:S(2)}) async-start(), calls=%async_computation.10 | async-start | bytes 2621440 | tf_op jit(solution)/shard_map/all_gather | solution.py:84
  7.9 174.8 %reduce-scatter.5.cloned.1.call-start = ((), (), s32[]{:S(2)}) async-start(), calls=%async_computation.4 | async-start | bytes 2621440 | tf_op jit(solution)/shard_map/reduce_scatter | solution.py:87
  60.7 5.8 slice-start
  110.1 6.0 copy-start.21
  112.4 3.8 copy-start.19
  112.4 6.1 slice-start.3
  116.2 1.5 copy-start.17
  116.2 2.4 slice-start.4
  117.7 0.8 copy-start.15
  120.6 6.1 copy-start.3
  120.6 6.1 copy-start.9
  128.1 8.1 copy-start.31
  136.2 2.6 copy-start.29
  136.3 46.4 %copy-start.4 = (bf16[1,128,2048]{2,1,0:T(8,128)(2,1)S(1)}, bf16[1,128,2048]{2,1,0:T(8,128)(2,1)}, u32[]{:S(2)}) copy-start(bf16[1,128,2048]{2,1,0:T(8,128)(2,1)} %param.14) | copy-start | bytes 1572868
  138.9 92.6 %all-gather.7.cloned.1.call-start = ((), (), s32[]{:S(2)}) async-start(), calls=%async_computation.5 | async-start | bytes 2621440 | tf_op jit(solution)/shard_map/all_gather | solution.py:84
  186.1 91.6 %all-gather.13.cloned.1.call-start = ((), (), s32[]{:S(2)}) async-start(), calls=%async_computation.11 | async-start | bytes 2621440 | tf_op jit(solution)/shard_map/all_gather | solution.py:84
  186.7 156.6 %reduce-scatter.9.cloned.1.call-start = ((), (), s32[]{:S(2)}) async-start(), calls=%async_computation.7 | async-start | bytes 2621440 | tf_op jit(solution)/shard_map/reduce_scatter | solution.py:87
  231.5 7.6 copy-start.24
  288.1 5.8 copy-start.35
  288.1 5.8 copy-start.34
  293.9 49.4 %copy-start.5 = (bf16[128,2048]{1,0:T(8,128)(2,1)S(1)}, bf16[128,2048]{1,0:T(8,128)(2,1)}, u32[]{:S(2)}) copy-start(bf16[128,2048]{1,0:T(8,128)(2,1)} %reduce-scatter.5.cloned.1.call-done) | copy-start | bytes 1572868
  300.6 92.2 %all-gather.9.cloned.1.call-start = ((), (), s32[]{:S(2)}) async-start(), calls=%async_computation.8 | async-start | bytes 2621440 | tf_op jit(solution)/shard_map/all_gather | solution.py:84
  347.4 212.1 %reduce-scatter.11.cloned.1.call-start = ((), (), s32[]{:S(2)}) async-start(), calls=%async_computation.9 | async-start | bytes 2621440 | tf_op jit(solution)/shard_map/reduce_scatter | solution.py:87
  396.5 8.2 copy-start.32
  396.5 8.2 copy-start.33
  404.8 4.9 slice-start.1
  404.8 5.8 slice-start.2
  410.6 2.5 copy-start.18
  413.2 2.0 copy-start.2
  413.2 2.0 copy-start.16
  415.2 1.6 copy-start.22
  416.8 1.6 copy-start.23
  418.4 1.6 copy-start.10
  422.7 178.5 %reduce-scatter.7.cloned.1.call-start = ((), (), s32[]{:S(2)}) async-start(), calls=%async_computation.6 | async-start | bytes 2621440 | tf_op jit(solution)/shard_map/reduce_scatter | solution.py:87
  430.3 388.8 %all-reduce.6.cloned.1.call-start = ((), (), s32[]{:S(2)}) async-start(), calls=%async_computation.12 | async-start | bytes 48234496 | tf_op jit(solution)/shard_map/psum | solution.py:131
  430.3 7.3 copy-start.25
  430.3 7.3 copy-start.36
  437.7 4.7 copy-start.26
  437.7 4.7 copy-start.37
  460.5 11.7 %copy-start.27 = (bf16[512,2048]{1,0:T(8,128)(2,1)S(1)}, bf16[512,2048]{1,0:T(8,128)(2,1)}, u32[]{:S(2)}) copy-start(bf16[512,2048]{1,0:T(8,128)(2,1)} %all-gather.9.cloned.1.call-done) | copy-start | bytes 6291460
  460.5 11.7 %copy-start.30 = (bf16[8,64,512]{2,1,0:T(8,128)(2,1)S(1)}, bf16[8,64,512]{2,1,0:T(8,128)(2,1)}, u32[]{:S(2)}) copy-start(bf16[8,64,512]{2,1,0:T(8,128)(2,1)} %copy-done.29) | copy-start | bytes 1572868
  472.1 2.6 copy-start.20
  537.6 7.7 copy-start.28
  537.6 63.6 %copy-start.7 = (bf16[128,2048]{1,0:T(8,128)(2,1)S(1)}, bf16[128,2048]{1,0:T(8,128)(2,1)}, u32[]{:S(2)}) copy-start(bf16[128,2048]{1,0:T(8,128)(2,1)} %reduce-scatter.9.cloned.1.call-done) | copy-start | bytes 1572868
  537.6 63.6 %copy-start.8 = (bf16[1,128,2048]{2,1,0:T(8,128)(2,1)S(1)}, bf16[1,128,2048]{2,1,0:T(8,128)(2,1)}, u32[]{:S(2)}) copy-start(bf16[1,128,2048]{2,1,0:T(8,128)(2,1)} %param.27) | copy-start | bytes 1572868
  819.1 7.9 copy-start.6
  819.1 12.8 %slice-start.5 = ((s8[5242880]{0:T(1024)(128)(4,1)}), s8[4194304]{0:T(1024)(128)(4,1)S(1)}, s32[]{:S(2)}) async-start(s8[5242880]{0:T(1024)(128)(4,1)} %bitcast.133), calls=%async_computation.18 | async-start | bytes 8388608
  827.0 4.9 slice-start.6
  831.9 5.5 copy-start.14
  837.4 2.6 copy-start.13
  840.0 2.6 copy-start.12
  842.7 2.6 copy-start.11
  845.3 2.5 copy-start.1
Sparse Core Ops, SparseCore 0:
  9.6 48.6 all-gather.10
  139.0 43.6 reduce-scatter.4
  186.2 45.2 all-gather.6
  233.0 44.6 all-gather.12
  300.8 42.4 reduce-scatter.8
  347.6 45.2 all-gather.8
  422.8 42.5 reduce-scatter.10
  468.4 43.1 reduce-scatter.6
  517.9 301.0 all-reduce.5
where the time goes:
time: 862 us; the launch traced here: 855 us
  waiting for transfers between devices  424 us (49%)
  local copies, waits for them, and re-layouts  161 us (19%)
  matrix products  118 us (14%)
  other arithmetic  68.6 us (8%)
  blocking collectives  67.3 us (8%)
  between operations  15.2 us (2%)
    psum x1, waiting for transfers between devices, total_sum(): return lax.psum(values.astype(jnp.bfloat16), 'replica').astype(jnp.float32)  215 us
    all_gather x4, waiting for transfers between devices, gather(): return lax.all_gather(values, 'group', axis=0, tiled=True)  121 us
    unnamed x95, local copies, waits for them, and re-layouts  93.4 us
    reduce_scatter x4, waiting for transfers between devices, scatter(): lax.psum_scatter(values.astype(jnp.bfloat16), 'group', scatter_dimension=...  86.4 us
    psum x1, blocking collectives, local(): lax.psum(jnp.stack([gain_one_grad, gain_two_grad]), ('replica', 'group'))  39.4 us
    dot_general x7, matrix products, cols_dot(): lax.dot_general(left, right, (((1,), (1,)), ((), ())), preferred_element_...  31.9 us
    reshape x1, local copies, waits for them, and re-layouts, fold_offsets(): flattened.reshape(block_heads, row_count, row_count + col_count + 1)  31.4 us
    dot_general x7, matrix products, plain_dot(): return jnp.dot(left, right, preferred_element_type=jnp.float32)  31 us
  transfers between devices with their start and end apart: 9, of which 6 were waited for; matrix products, arithmetic and copies ran while one was open for 26% of the time, Pallas kernels for 0%

commit v1 on v0

--- a/solution.py
+++ b/solution.py
@@ -1,3 +1,4 @@
+import functools
 import jax
 import jax.numpy as jnp
 from jax import lax
@@ -7,6 +8,13 @@
 negative = -1000000000.0
 highest = lax.Precision.HIGHEST
 head_dim = 64
+
+
+def begin_marks_up(xin, ax_name):
+    return lax.all_gather(xin, ax_name).sum(axis=0)
+
+
+cover_roots = functools.partial(begin_marks_up, ax_name="replica")
 
 
 def rms_scale(values, gain):
@@ -128,7 +136,7 @@
     up_grad = rows_dot(normed_two, grad_up)
 
     def total_sum(values):
-        return lax.psum(values.astype(jnp.bfloat16), "replica").astype(jnp.float32)
+        return cover_roots(values.astype(jnp.bfloat16)).astype(jnp.float32)
 
     ffn_out_grad, gate_grad, up_grad = (
         total_sum(ffn_out_grad),

time: 862 us -> 1530 us (1.77)
  waiting for transfers between devices: 424 us -> 976 us
  other arithmetic: 68.6 us -> 170 us
    all_gather x0 -> x7, waiting for transfers between devices: none -> 767 us  [begin_marks_up(): return lax.all_gather(xin, ax_name).sum(axis=0)]
    psum x1 -> x0, waiting for transfers between devices: 215 us -> none  [total_sum(): return lax.psum(values.astype(jnp.bfloat16), 'replica').astype(jnp.float32)]
    reduce_sum x0 -> x7, other arithmetic: none -> 99.3 us  [begin_marks_up(): return lax.all_gather(xin, ax_name).sum(axis=0)]
    unnamed x95 -> x79, local copies, waits for them, and re-layouts: 93.4 us -> 95.3 us
  transfers between devices with their start and end apart: 9 -> 15, of which waited for: 6 -> 11; matrix products, arithmetic and copies ran while one was open for 26% -> 21% of each run, Pallas kernels for 0% -> 0%
where the time goes in v1:
time: 1530 us; the launch traced here: 1520 us
  waiting for transfers between devices  976 us (64%)
  other arithmetic  170 us (11%)
  local copies, waits for them, and re-layouts  163 us (11%)
  matrix products  125 us (8%)
  blocking collectives  68 us (4%)
  between operations  15.5 us (1%)
    all_gather x7, waiting for transfers between devices, begin_marks_up(): return lax.all_gather(xin, ax_name).sum(axis=0)  767 us
    all_gather x4, waiting for transfers between devices, gather(): return lax.all_gather(values, 'group', axis=0, tiled=True)  121 us
    reduce_sum x7, other arithmetic, begin_marks_up(): return lax.all_gather(xin, ax_name).sum(axis=0)  99.3 us
    unnamed x79, local copies, waits for them, and re-layouts  95.3 us
    reduce_scatter x4, waiting for transfers between devices, scatter(): lax.psum_scatter(values.astype(jnp.bfloat16), 'group', scatter_dimension=...  86.4 us
    psum x1, blocking collectives, local(): lax.psum(jnp.stack([gain_one_grad, gain_two_grad]), ('replica', 'group'))  39.1 us
    dot_general x7, matrix products, rows_dot(): lax.dot_general(left, right, (((0,), (0,)), ((), ())), preferred_element_...  35.8 us
    dot_general x7, matrix products, cols_dot(): lax.dot_general(left, right, (((1,), (1,)), ((), ())), preferred_element_...  31.9 us
  transfers between devices with their start and end apart: 15, of which 11 were waited for; matrix products, arithmetic and copies ran while one was open for 21% of the time, Pallas kernels for 0%

profile of v1, /device:TPU:0, one launch (start us, length us, event | category | flops | bytes accessed | tf_op | source)
XLA Modules:
  0.0 1519.6 jit_solution(12938002518708547528)
XLA Ops:
  11.1 7.7 broadcast_in_dim.67
  18.8 25.5 %reshape.157 = f32[4198400]{0:T(1024)} reshape(f32[8,512,1025]{2,1,0:T(8,128)} %broadcast_in_dim.67) | data formatting | bytes 33587200
  44.3 16.5 %reshape.135 = f32[8,524800]{1,0:T(8,128)} reshape(f32[4198400]{0:T(1024)} %reshape.157) | data formatting | bytes 33587200 | tf_op jit(solution)/shard_map/reshape | solution.py:48
  60.8 5.8 slice-done
  66.6 16.0 %copy.45 = f32[1,8,512,1024]{3,2,1,0:T(8,128)S(1)} copy(f32[1,8,512,1024]{3,1,2,0:T(8,128)S(1)} %bitcast.133) | data formatting | bytes 33554432
  82.6 4.4 slice.30
  87.0 9.1 copy.40
  96.1 14.0 all_gather.58
  112.3 3.8 convolution_convert_fusion.13
  120.7 5.0 fusion.52
  129.0 8.0 fusion.15
  137.1 2.6 convolution_convert_fusion.8
  139.7 43.8 %reduce-scatter.5.cloned.1.call-done = bf16[128,2048]{1,0:T(8,128)(2,1)} async-done(((bf16[512,2048]{1,0:T(8,128)(2,1)}), bf16[128,2048]{1,0:T(8,128)(2,1)}) %reduce-scatter.5.cloned.1.call-update) | async-done | bytes 524304 | tf_op jit(solution)/shard_map/reduce_scatter | solution.py:95
  187.7 44.6 %all-gather.21.cloned.1.call-done = bf16[512,2048]{1,0:T(8,128)(2,1)} async-done(((bf16[128,2048]{1,0:T(8,128)(2,1)}), bf16[512,2048]{1,0:T(8,128)(2,1)}) %all-gather.21.cloned.1.call-update) | async-done | bytes 2097168 | tf_op jit(solution)/shard_map/all_gather | solution.py:92
  232.3 7.6 fusion.54
  239.9 7.1 fusion.53
  247.0 31.5 %all-gather.27.cloned.1.call-done = bf16[1,512,2048]{2,1,0:T(8,128)(2,1)} async-done(((bf16[1,128,2048]{2,1,0:T(8,128)(2,1)}), bf16[1,512,2048]{2,1,0:T(8,128)(2,1)}) %all-gather.27.cloned.1.call-update) | async-done | bytes 2097168 | tf_op jit(solution)/shard_map/all_gather | solution.py:92
  278.5 10.3 multiply_convert_fusion.1
  288.8 5.8 fusion.55
  294.7 6.7 add_convert_fusion.1
  301.5 42.6 %reduce-scatter.9.cloned.1.call-done = bf16[128,2048]{1,0:T(8,128)(2,1)} async-done(((bf16[512,2048]{1,0:T(8,128)(2,1)}), bf16[128,2048]{1,0:T(8,128)(2,1)}) %reduce-scatter.9.cloned.1.call-update) | async-done | bytes 524304 | tf_op jit(solution)/shard_map/reduce_scatter | solution.py:95
  348.5 45.2 %all-gather.23.cloned.1.call-done = bf16[512,2048]{1,0:T(8,128)(2,1)} async-done(((bf16[128,2048]{1,0:T(8,128)(2,1)}), bf16[512,2048]{1,0:T(8,128)(2,1)}) %all-gather.23.cloned.1.call-update) | async-done | bytes 2097168 | tf_op jit(solution)/shard_map/all_gather | solution.py:92
  393.6 3.7 convolution_convert_fusion.11
  397.3 8.2 fusion.18
  405.5 4.8 multiply_reduce_fusion
  420.3 2.7 add_convert_fusion
  423.5 7.1 convolution_convert_fusion.7
  430.8 4.2 convolution_convert_fusion.3
  435.0 4.4 convolution_convert_fusion.4
  439.5 4.5 convolution_convert_fusion.5
  444.0 4.6 convolution_convert_fusion.6
  448.6 6.3 convolution_convert_fusion
  456.6 6.0 convolution_convert_fusion.1
  462.8 6.0 convolution_convert_fusion.2
  468.8 6.5 copy.41
  475.3 6.7 pad_bitcast_fusion
  482.0 11.5 copy.43
  493.6 9.9 pad_convert_fusion
  503.5 12.8 reshape.159
  516.3 30.8 %reshape.144 = f32[8,512,1025]{2,1,0:T(8,128)} reshape(f32[4198400]{0:T(1024)} %reshape.159) | data formatting | bytes 33587200 | tf_op jit(solution)/shard_map/reshape | solution.py:60
  547.1 7.4 reduce_sum.207
  554.9 14.8 psum.15
  571.3 39.1 %psum.14 = f32[2,2048]{1,0:T(2,128)S(1)} all-reduce(f32[2,2048]{1,0:T(2,128)S(1)} %pad_maximum_fusion), channel_id=1, replica_groups=mesh['replica'=8,'group'=4] {'replica','group'}, use_global_device_ids=true, to_apply=%region_14.15 | all-reduce | flops 4096 | bytes 32768 | tf_op jit(solution)/shard_map/psum | solution.py:193
  611.2 3.2 fusion.34
  614.4 10.0 reduce_sum.206
  624.4 2.5 convert_element_type.224
  626.9 68.8 %all-gather.33.cloned.1.call-done = bf16[16384,512]{1,0:T(8,128)(2,1)} async-done(((bf16[2048,512]{1,0:T(8,128)(2,1)}), bf16[16384,512]{1,0:T(8,128)(2,1)}) %all-gather.33.cloned.1.call-update) | async-done | bytes 16777232 | tf_op jit(solution)/shard_map/all_gather | solution.py:14
  695.7 9.3 reduce_sum.205
  705.0 2.6 convert_element_type.222
  707.6 79.8 %all-gather.31.cloned.1.call-done = bf16[16384,512]{1,0:T(8,128)(2,1)} async-done(((bf16[2048,512]{1,0:T(8,128)(2,1)}), bf16[16384,512]{1,0:T(8,128)(2,1)}) %all-gather.31.cloned.1.call-update) | async-done | bytes 16777232 | tf_op jit(solution)/shard_map/all_gather | solution.py:14
  787.5 9.4 reduce_sum.204
  796.9 82.2 %all-gather.29.cloned.1.call-done = bf16[16384,512]{1,0:T(8,128)(2,1)} async-done(((bf16[2048,512]{1,0:T(8,128)(2,1)}), bf16[16384,512]{1,0:T(8,128)(2,1)}) %all-gather.29.cloned.1.call-update) | async-done | bytes 16777232 | tf_op jit(solution)/shard_map/all_gather | solution.py:14
  879.1 10.9 reduce_sum.203
  890.0 4.8 convert_element_type.218
  894.7 3.4 convert_element_type.220
  898.1 180.1 %all-gather.41.cloned.1.call-done = bf16[10240,2048]{1,0:T(8,128)(2,1)} async-done(((bf16[1280,2048]{1,0:T(8,128)(2,1)}), bf16[10240,2048]{1,0:T(8,128)(2,1)}) %all-gather.41.cloned.1.call-update) | async-done | bytes 41943056 | tf_op jit(solution)/shard_map/all_gather | solution.py:14
  1078.2 21.0 %reduce_sum.210 = bf16[1280,2048]{1,0:T(8,128)(2,1)} reduce(bf16[8,1280,2048]{2,1,0:T(8,128)(2,1)} %bitcast.134, bf16[]{:T(256)} %constant.48.clone.1), dimensions={0}, to_apply=%region_23.24 | reduce | flops 18350080 | bytes 47185920 | tf_op jit(solution)/shard_map/reduce_sum | solution.py:14
  1099.1 178.0 %all-gather.39.cloned.1.call-done = bf16[16384,1280]{1,0:T(8,128)(2,1)} async-done(((bf16[2048,1280]{1,0:T(8,128)(2,1)}), bf16[16384,1280]{1,0:T(8,128)(2,1)}) %all-gather.39.cloned.1.call-update) | async-done | bytes 41943056 | tf_op jit(solution)/shard_map/all_gather | solution.py:14
  1277.1 21.0 %reduce_sum.209 = bf16[2048,1280]{1,0:T(8,128)(2,1)} reduce(bf16[8,2048,1280]{2,1,0:T(8,128)(2,1)} %bitcast.135, bf16[]{:T(256)} %constant.48.clone.1), dimensions={0}, to_apply=%region_22.23 | reduce | flops 18350080 | bytes 47185920 | tf_op jit(solution)/shard_map/reduce_sum | solution.py:14
  1298.1 178.5 %all-gather.37.cloned.1.call-done = bf16[16384,1280]{1,0:T(8,128)(2,1)} async-done(((bf16[2048,1280]{1,0:T(8,128)(2,1)}), bf16[16384,1280]{1,0:T(8,128)(2,1)}) %all-gather.37.cloned.1.call-update) | async-done | bytes 41943056 | tf_op jit(solution)/shard_map/all_gather | solution.py:14
  1476.6 17.7 %reduce_sum.208 = bf16[2048,1280]{1,0:T(8,128)(2,1)} reduce(bf16[8,2048,1280]{2,1,0:T(8,128)(2,1)} %bitcast.136, bf16[]{:T(256)} %constant.48.clone.1), dimensions={0}, to_apply=%region_21.22 | reduce | flops 18350080 | bytes 47185920 | tf_op jit(solution)/shard_map/reduce_sum | solution.py:14
  1494.3 7.9 convert_element_type.226
  1502.2 4.9 convert_element_type.228
  1507.1 5.5 convert_element_type.230
  (140 shorter events, 37.0 us)
Async XLA Ops:
  7.2 129.9 %copy-start = (bf16[512,2048]{1,0:T(8,128)(2,1)S(1)}, bf16[512,2048]{1,0:T(8,128)(2,1)}, u32[]{:S(2)}) copy-start(bf16[512,2048]{1,0:T(8,128)(2,1)} %param.21) | copy-start | bytes 6291460
  7.2 103.0 %all-gather.25.cloned.1.call-start = ((), (), s32[]{:S(2)}) async-start(), calls=%async_computation.10 | async-start | bytes 2621440 | tf_op jit(solution)/shard_map/all_gather | solution.py:92
  7.9 175.6 %reduce-scatter.5.cloned.1.call-start = ((), (), s32[]{:S(2)}) async-start(), calls=%async_computation.4 | async-start | bytes 2621440 | tf_op jit(solution)/shard_map/reduce_scatter | solution.py:95
  60.8 5.8 slice-start
  112.3 3.8 copy-start.15
  112.3 3.8 copy-start.16
  112.3 6.1 slice-start.3
  116.1 1.5 copy-start.13
  116.1 2.6 slice-start.4
  117.6 0.8 copy-start.11
  120.7 6.1 copy-start.3
  120.7 6.1 copy-start.9
  128.2 0.8 copy-start.24
  137.0 47.8 %copy-start.22 = (bf16[8,64,512]{2,1,0:T(8,128)(2,1)}, bf16[8,64,512]{2,1,0:T(8,128)(2,1)S(1)}, u32[]{:S(2)}) copy-start(bf16[8,64,512]{2,1,0:T(8,128)(2,1)S(1)} %fusion.15) | copy-start | bytes 1572868
  137.0 46.5 %copy-start.4 = (bf16[1,128,2048]{2,1,0:T(8,128)(2,1)S(1)}, bf16[1,128,2048]{2,1,0:T(8,128)(2,1)}, u32[]{:S(2)}) copy-start(bf16[1,128,2048]{2,1,0:T(8,128)(2,1)} %param.14) | copy-start | bytes 1572868
  139.7 92.6 %all-gather.21.cloned.1.call-start = ((), (), s32[]{:S(2)}) async-start(), calls=%async_computation.5 | async-start | bytes 2621440 | tf_op jit(solution)/shard_map/all_gather | solution.py:92
  186.9 91.6 %all-gather.27.cloned.1.call-start = ((), (), s32[]{:S(2)}) async-start(), calls=%async_computation.11 | async-start | bytes 2621440 | tf_op jit(solution)/shard_map/all_gather | solution.py:92
  187.5 156.6 %reduce-scatter.9.cloned.1.call-start = ((), (), s32[]{:S(2)}) async-start(), calls=%async_computation.7 | async-start | bytes 2621440 | tf_op jit(solution)/shard_map/reduce_scatter | solution.py:95
  232.3 7.6 copy-start.19
  288.8 5.8 copy-start.28
  288.8 5.8 copy-start.27
  294.7 49.4 %copy-start.6 = (bf16[128,2048]{1,0:T(8,128)(2,1)S(1)}, bf16[128,2048]{1,0:T(8,128)(2,1)}, u32[]{:S(2)}) copy-start(bf16[128,2048]{1,0:T(8,128)(2,1)} %reduce-scatter.5.cloned.1.call-done) | copy-start | bytes 1572868
  301.4 92.2 %all-gather.23.cloned.1.call-start = ((), (), s32[]{:S(2)}) async-start(), calls=%async_computation.8 | async-start | bytes 2621440 | tf_op jit(solution)/shard_map/all_gather | solution.py:92
  348.2 221.5 %reduce-scatter.11.cloned.1.call-start = ((), (), s32[]{:S(2)}) async-start(), calls=%async_computation.9 | async-start | bytes 2621440 | tf_op jit(solution)/shard_map/reduce_scatter | solution.py:95
  397.3 8.2 copy-start.25
  397.3 8.2 copy-start.26
  405.5 4.9 slice-start.1
  405.5 5.8 slice-start.2
  411.4 2.5 copy-start.14
  413.9 2.2 copy-start.2
  413.9 1.4 copy-start.12
  413.9 3.3 copy-start.17
  417.2 1.6 copy-start.18
  418.7 1.6 copy-start.10
  423.1 188.1 %reduce-scatter.7.cloned.1.call-start = ((), (), s32[]{:S(2)}) async-start(), calls=%async_computation.6 | async-start | bytes 2621440 | tf_op jit(solution)/shard_map/reduce_scatter | solution.py:95
  423.5 7.2 copy-start.23
  430.7 183.7 %all-gather.35.cloned.1.call-start = ((), (), s32[]{:S(2)}) async-start(), calls=%async_computation.15 | async-start | bytes 18874368 | tf_op jit(solution)/shard_map/all_gather | solution.py:14
  435.0 260.7 %all-gather.33.cloned.1.call-start = ((), (), s32[]{:S(2)}) async-start(), calls=%async_computation.14 | async-start | bytes 18874368 | tf_op jit(solution)/shard_map/all_gather | solution.py:14
  439.4 348.1 %all-gather.31.cloned.1.call-start = ((), (), s32[]{:S(2)}) async-start(), calls=%async_computation.13 | async-start | bytes 18874368 | tf_op jit(solution)/shard_map/all_gather | solution.py:14
  443.9 4.7 copy-start.29
  444.0 435.2 %all-gather.29.cloned.1.call-start = ((), (), s32[]{:S(2)}) async-start(), calls=%async_computation.12 | async-start | bytes 18874368 | tf_op jit(solution)/shard_map/all_gather | solution.py:14
  448.6 629.6 %all-gather.41.cloned.1.call-start = ((), (), s32[]{:S(2)}) async-start(), calls=%async_computation.18 | async-start | bytes 47185920 | tf_op jit(solution)/shard_map/all_gather | solution.py:14
  455.0 1.6 copy-start.20
  455.0 822.1 %all-gather.39.cloned.1.call-start = ((), (), s32[]{:S(2)}) async-start(), calls=%async_computation.17 | async-start | bytes 47185920 | tf_op jit(solution)/shard_map/all_gather | solution.py:14
  462.6 1014.0 %all-gather.37.cloned.1.call-start = ((), (), s32[]{:S(2)}) async-start(), calls=%async_computation.16 | async-start | bytes 47185920 | tf_op jit(solution)/shard_map/all_gather | solution.py:14
  547.1 7.4 copy-start.21
  547.1 64.1 %copy-start.7 = (bf16[128,2048]{1,0:T(8,128)(2,1)S(1)}, bf16[128,2048]{1,0:T(8,128)(2,1)}, u32[]{:S(2)}) copy-start(bf16[128,2048]{1,0:T(8,128)(2,1)} %reduce-scatter.9.cloned.1.call-done) | copy-start | bytes 1572868
  547.1 64.1 %copy-start.8 = (bf16[1,128,2048]{2,1,0:T(8,128)(2,1)S(1)}, bf16[1,128,2048]{2,1,0:T(8,128)(2,1)}, u32[]{:S(2)}) copy-start(bf16[1,128,2048]{2,1,0:T(8,128)(2,1)} %param.27) | copy-start | bytes 1572868
  1494.3 7.9 copy-start.5
  1494.3 12.8 slice-start.5
  1502.2 4.9 slice-start.6
  1502.2 10.4 copy-start.1
Sparse Core Ops, SparseCore 0:
  9.6 48.6 all-gather.24
  139.8 43.6 reduce-scatter.4
  187.0 45.2 all-gather.20
  233.8 44.6 all-gather.26
  301.5 42.4 reduce-scatter.8
  348.3 45.2 all-gather.22
  423.2 42.5 reduce-scatter.10
  468.8 43.1 reduce-scatter.6
  513.9 90.1 all-gather.34
  605.8 89.8 all-gather.32
  697.6 89.8 all-gather.30
  789.2 89.8 all-gather.28
  881.0 197.1 all-gather.40
  1079.9 197.1 all-gather.38
  1279.4 197.1 all-gather.36
